TPU v7x, 256 devices: a whole 4x4x8 slice. The times are simulated.
256 devices in a mesh: dp: 8 (over x, z_hi), pipe: 4 (over z_lo), expert: 8 (over y, core).
Axes of the slice: x: 4, y: 4, z: 8 (z_hi: 2, z_lo: 4; z = z_hi * 4 + z_lo), core: 2. Of those that a mesh axis runs over, the one named last changes fastest.
Arguments:
- tokens: bfloat16 [8192, 2048], P(('dp', 'expert')), may hold values from -6 to 6
- cotangent: bfloat16 [8192, 2048], P(('dp', 'expert')), may hold values from -6 to 6
- owner_ids: int32 [4, 8192, 4], P('pipe', ('dp', 'expert')), may hold values from 0 to 63, all different within a row; in each aligned block of 32 rows (0 to 31, 32 to 63, ..., all dimensions but the last counted through in order) at most 3 rows name the same one
- gate_weights: bfloat16 [4, 8192, 4], P('pipe', ('dp', 'expert')), may hold values from 0.049804688 to 0.25
- norm_gain: float32 [4, 2048], P('pipe'), may hold values from 0.5 to 1.5
- w_gate: bfloat16 [4, 64, 2048, 384], P('pipe', ('dp', 'expert')), may hold values from -0.125 to 0.125
- w_up: bfloat16 [4, 64, 2048, 384], P('pipe', ('dp', 'expert')), may hold values from -0.125 to 0.125
- w_down: bfloat16 [4, 64, 384, 2048], P('pipe', ('dp', 'expert')), may hold values from -0.3125 to 0.3125
Outputs:
- segment_out: bfloat16 [4, 8192, 2048], P('pipe', ('dp', 'expert'))
- segment_grad: bfloat16 [4, 8192, 2048], P('pipe', ('dp', 'expert'))
- gain_grad: float32 [4, 2048], P('pipe')
Inputs may be any that keep to these rules, and one draw needn't show every extreme that they name: `owner_ids`: each row names 4 different owners. In each aligned block of 32 rows (layers in order, then tokens) no owner is named by more than 3 rows, and that bound is reached.
All inputs are finite; a program needn't handle non-finite values.
Results may differ from a plain program's by a relative error of at most 0.014.
Values may be sent and summed in bfloat16 or wider, within the bound.
A program may use at most 128 MiB of HBM per device.

v0:
```python
import jax
import jax.numpy as jnp
from jax import lax
from jax.sharding import PartitionSpec as P

MICRO = 4
epsilon = 1e-06


def from_behind(value, axis, steps):
    count = lax.axis_size(axis)
    leading, last = (max(0, -steps), min(count, count - steps))
    return lax.ppermute(value, axis, [(source, source + steps) for source in range(leading, last)])


def inverse_rms(values):
    return lax.rsqrt(jnp.mean(values * values, axis=-1, keepdims=True) + epsilon)


def contract_last(left, right):
    return lax.dot_general(
        left, right, (((1,), (1,)), ((), ())), preferred_element_type=jnp.float32
    )


def route_tables(ids_part, owners, capacity):
    owner_range = jnp.arange(owners, dtype=jnp.int32)
    onehot = (ids_part[:, :, None] == owner_range[None, None, :]).astype(jnp.int32)
    member = jnp.sum(onehot, axis=1)
    position = jnp.cumsum(member, axis=0) - member
    slot_range = jnp.arange(capacity, dtype=jnp.int32)
    placed = (position[:, :, None] == slot_range[None, None, :]) & (member[:, :, None] > 0)
    placing = jnp.transpose(placed, (1, 2, 0)).astype(jnp.bfloat16)
    return (onehot.astype(jnp.float32), placing)


def gate_slots(onehot, gates_part, placing, experts_here):
    gate_pairs = gates_part.astype(jnp.float32).reshape(gates_part.shape[0], -1, experts_here)
    chosen = jnp.einsum("rjo,rjc->roc", onehot, gate_pairs)
    return jnp.einsum("okr,roc->okc", placing.astype(jnp.float32), chosen).astype(jnp.bfloat16)


def send_rows(row_block, pair_block):
    got_rows, got_pairs = (
        lax.all_to_all(row_block, ("dp", "expert"), split_axis=0, concat_axis=0, tiled=True),
        lax.all_to_all(pair_block, ("dp", "expert"), split_axis=0, concat_axis=0, tiled=True),
    )
    return (got_rows, got_pairs)


def return_rows(row_block):
    return lax.all_to_all(row_block, ("dp", "expert"), split_axis=0, concat_axis=0, tiled=True)


def send_grads(row_block):
    return lax.all_to_all(row_block, ("dp", "expert"), split_axis=0, concat_axis=0, tiled=True)


def return_grads(row_block):
    return lax.all_to_all(row_block, ("dp", "expert"), split_axis=0, concat_axis=0, tiled=True)


def expert_forward(flat_rows, flat_pairs, joint_mats, down_mats):
    hidden_width = down_mats.shape[1]
    joint_pre = jnp.dot(flat_rows, joint_mats[0], preferred_element_type=jnp.float32)
    gate_pre = joint_pre[:, :hidden_width]
    up_pre = joint_pre[:, hidden_width:]
    hidden = (jax.nn.silu(gate_pre) * up_pre).astype(jnp.bfloat16)
    projected = jnp.dot(hidden, down_mats[0], preferred_element_type=jnp.float32)
    term = flat_pairs.astype(jnp.float32) * projected
    kept_both = [joint_pre]
    return (term.astype(jnp.bfloat16), jnp.stack(kept_both))


def expert_backward(grad_rows, flat_pairs, joint_keep, joint_mats, down_mats):
    hidden_width = down_mats.shape[1]
    q_vals = contract_last(grad_rows, down_mats[0])
    gate_pre = joint_keep[0][:, :hidden_width]
    up_pre = joint_keep[0][:, hidden_width:]
    sigma = jax.nn.sigmoid(gate_pre)
    weight = flat_pairs.astype(jnp.float32)
    d_gate = (q_vals * weight * up_pre * sigma * (1.0 + gate_pre * (1.0 - sigma))).astype(
        jnp.bfloat16
    )
    d_up = (q_vals * weight * gate_pre * sigma).astype(jnp.bfloat16)
    joint_grad = jnp.concatenate([d_gate, d_up], axis=1)
    term = contract_last(joint_grad, joint_mats[0])
    return term.astype(jnp.bfloat16)


def body(tokens, cotangent, owner_ids, gate_weights, norm_gain, w_gate, w_up, w_down):
    segments = lax.axis_size("pipe")
    segment_index = lax.axis_index("pipe")
    owners = lax.axis_size("dp") * lax.axis_size("expert")
    tok_rows = tokens.shape[0]
    width = tokens.shape[1]
    micro_rows = tok_rows // MICRO
    route_count = owner_ids.shape[2]
    capacity = max(2, (5 * micro_rows * route_count + 4 * owners - 1) // (4 * owners))
    slot_count = owners * capacity
    gain_row = norm_gain[0]
    joint_mats = jnp.concatenate([w_gate[0], w_up[0]], axis=2)
    down_mats = w_down[0]
    layer_ids = owner_ids[0]
    layer_gates = gate_weights[0]
    experts_here = joint_mats.shape[0]
    joint_width = joint_mats.shape[2]

    def skip_forward(operands):
        return (
            jnp.zeros((slot_count, width), jnp.bfloat16),
            jnp.zeros((experts_here, slot_count, joint_width), jnp.float32),
        )

    def run_forward(operands):
        return expert_forward(operands[0], operands[1], joint_mats, down_mats)

    def skip_backward(operands):
        return jnp.zeros((slot_count, width), jnp.bfloat16)

    def run_backward(operands):
        return expert_backward(operands[0], operands[1], operands[2], joint_mats, down_mats)

    def timing(micro):
        is_valid = (micro >= 0) & (micro < MICRO)
        slot_pick = jnp.where(is_valid, micro, MICRO)
        start_row = jnp.clip(micro, 0, MICRO - 1) * micro_rows
        return (is_valid, slot_pick, start_row)

    layer_outs = jnp.zeros((MICRO + 1, micro_rows, width), jnp.bfloat16)
    layer_ins = jnp.zeros((MICRO + 1, micro_rows, width), jnp.bfloat16)
    kept_joint = jnp.zeros((MICRO + 1, experts_here, slot_count, joint_width), jnp.float32)
    kept_pairs = jnp.zeros((MICRO + 1, slot_count, experts_here), jnp.bfloat16)
    grad_outs = jnp.zeros((MICRO + 1, micro_rows, width), jnp.bfloat16)
    gain_sum = jnp.zeros((width,), jnp.float32)
    ticks = MICRO + segments - 1
    incoming = jnp.zeros((micro_rows, width), jnp.bfloat16)
    for tick_num in range(ticks):
        forward_is_valid, forward_slot_pick, forward_start_row = timing(tick_num - segment_index)
        forward_own_part = lax.dynamic_slice_in_dim(tokens, forward_start_row, micro_rows, 0)
        forward_layer_in = jnp.where(segment_index == 0, forward_own_part, incoming)
        forward_ids_part = lax.dynamic_slice_in_dim(layer_ids, forward_start_row, micro_rows, 0)
        gates_part = lax.dynamic_slice_in_dim(layer_gates, forward_start_row, micro_rows, 0)
        forward_x_float = forward_layer_in.astype(jnp.float32)
        forward_scale = inverse_rms(forward_x_float)
        normed = (forward_x_float * forward_scale * gain_row).astype(jnp.bfloat16)
        forward_onehot, forward_placing = route_tables(forward_ids_part, owners, capacity)
        row_block = jnp.einsum(
            "okr,rd->okd", forward_placing, normed, preferred_element_type=jnp.float32
        ).astype(jnp.bfloat16)
        pair_block = gate_slots(forward_onehot, gates_part, forward_placing, experts_here)
        f_valid, f_pick, layer_in, x_float, f_placing, row_block, pair_block = (
            forward_is_valid,
            forward_slot_pick,
            forward_layer_in,
            forward_x_float,
            forward_placing,
            row_block,
            pair_block,
        )
        got_rows, got_pairs = send_rows(row_block, pair_block)
        flat_rows = got_rows.reshape(slot_count, width)
        flat_pairs = got_pairs.reshape(slot_count, experts_here)
        result, joint_pre = lax.cond(f_valid, run_forward, skip_forward, (flat_rows, flat_pairs))
        returned = return_rows(result.reshape(owners, capacity, width))
        branch = jnp.einsum("okr,okd->rd", f_placing, returned, preferred_element_type=jnp.float32)
        layer_out = (x_float + branch).astype(jnp.bfloat16)
        layer_outs = lax.dynamic_update_index_in_dim(layer_outs, layer_out, f_pick, 0)
        layer_ins = lax.dynamic_update_index_in_dim(layer_ins, layer_in, f_pick, 0)
        kept_joint = lax.dynamic_update_index_in_dim(kept_joint, joint_pre, f_pick, 0)
        kept_pairs = lax.dynamic_update_index_in_dim(kept_pairs, flat_pairs, f_pick, 0)
        if tick_num + 1 < ticks:
            incoming = from_behind(layer_out, "pipe", 1)
    incoming = jnp.zeros((micro_rows, width), jnp.bfloat16)
    for tick_num in range(ticks):
        backward_is_valid, backward_slot_pick, backward_start_row = timing(
            tick_num - (segments - 1 - segment_index)
        )
        own_part = lax.dynamic_slice_in_dim(cotangent, backward_start_row, micro_rows, 0)
        backward_grad_in = jnp.where(segment_index == segments - 1, own_part, incoming)
        ids_part = lax.dynamic_slice_in_dim(layer_ids, backward_start_row, micro_rows, 0)
        backward_layer_in = lax.dynamic_index_in_dim(
            layer_ins, backward_slot_pick, 0, keepdims=False
        )
        backward_x_float = backward_layer_in.astype(jnp.float32)
        backward_scale = inverse_rms(backward_x_float)
        onehot, backward_placing = route_tables(ids_part, owners, capacity)
        grad_block = jnp.einsum(
            "okr,rd->okd", backward_placing, backward_grad_in, preferred_element_type=jnp.float32
        ).astype(jnp.bfloat16)
        b_valid, b_pick, grad_in, bx_float, b_scale, b_placing, grad_block = (
            backward_is_valid,
            backward_slot_pick,
            backward_grad_in,
            backward_x_float,
            backward_scale,
            backward_placing,
            grad_block,
        )
        got_grads = send_grads(grad_block).reshape(slot_count, width)
        joint_keep = lax.dynamic_index_in_dim(kept_joint, b_pick, 0, keepdims=False)
        pair_keep = lax.dynamic_index_in_dim(kept_pairs, b_pick, 0, keepdims=False)
        owner_grad = lax.cond(
            b_valid, run_backward, skip_backward, (got_grads, pair_keep, joint_keep)
        )
        returned = return_grads(owner_grad.reshape(owners, capacity, width))
        normed_grad = jnp.einsum(
            "okr,okd->rd", b_placing, returned, preferred_element_type=jnp.float32
        )
        weighted = gain_row * normed_grad
        grad_x = (
            grad_in.astype(jnp.float32)
            + b_scale * weighted
            - bx_float
            * b_scale
            * b_scale
            * b_scale
            * jnp.mean(weighted * bx_float, axis=-1, keepdims=True)
        )
        gain_term = jnp.where(b_valid, jnp.sum(normed_grad * bx_float * b_scale, axis=0), 0.0)
        grad_bf, gain_term = (grad_x.astype(jnp.bfloat16), gain_term)
        grad_outs = lax.dynamic_update_index_in_dim(grad_outs, grad_bf, b_pick, 0)
        gain_sum = gain_sum + gain_term
        if tick_num + 1 < ticks:
            incoming = from_behind(grad_bf, "pipe", -1)
    gain_grad = lax.psum(gain_sum, ("dp", "expert"))
    segment_out = layer_outs[:MICRO].reshape(1, tok_rows, width)
    segment_grad = grad_outs[:MICRO].reshape(1, tok_rows, width)
    return (segment_out, segment_grad, gain_grad.reshape(1, width))


def solution(mesh):
    in_specs = (
        P(("dp", "expert"), None),
        P(("dp", "expert"), None),
        P("pipe", ("dp", "expert"), None),
        P("pipe", ("dp", "expert"), None),
        P("pipe", None),
        P("pipe", ("dp", "expert"), None, None),
        P("pipe", ("dp", "expert"), None, None),
        P("pipe", ("dp", "expert"), None, None),
    )
    out_specs = (
        P("pipe", ("dp", "expert"), None),
        P("pipe", ("dp", "expert"), None),
        P("pipe", None),
    )
    return jax.shard_map(body, mesh=mesh, in_specs=in_specs, out_specs=out_specs, check_vma=False)
```

profile of v0, /device:TPU:1, one launch (start us, length us, event | category | flops | bytes accessed | tf_op | source)
XLA Modules:
  0.0 1507.8 jit_solution(17595029229092546663)
XLA Ops:
  40.4 25.5 %all-to-all-done.1 = bf16[64,3,2048]{2,1,0:T(4,128)(2,1)} async-done(((bf16[64,3,2048]{2,1,0:T(4,128)(2,1)}), bf16[64,3,2048]{2,1,0:T(4,128)(2,1)}, u32[]{:S(2)}, u32[]{:S(2)}) %all-to-all-start.1) | async-done | bytes 786464 | tf_op jit(solution)/shard_map/all_to_all | solution.py:45
  136.9 28.5 %all-to-all-done.4 = bf16[64,3,2048]{2,1,0:T(4,128)(2,1)} async-done(((bf16[64,3,2048]{2,1,0:T(4,128)(2,1)}), bf16[64,3,2048]{2,1,0:T(4,128)(2,1)}, u32[]{:S(2)}, u32[]{:S(2)}) %all-to-all-start.4) | async-done | bytes 786464 | tf_op jit(solution)/shard_map/all_to_all | solution.py:45
  246.7 28.6 %all-to-all-done.7 = bf16[64,3,2048]{2,1,0:T(4,128)(2,1)} async-done(((bf16[64,3,2048]{2,1,0:T(4,128)(2,1)}), bf16[64,3,2048]{2,1,0:T(4,128)(2,1)}, u32[]{:S(2)}, u32[]{:S(2)}) %all-to-all-start.7) | async-done | bytes 786464 | tf_op jit(solution)/shard_map/all_to_all | solution.py:45
  298.6 20.2 %all-to-all-done.8 = bf16[64,3,2048]{2,1,0:T(4,128)(2,1)} async-done(((bf16[64,3,2048]{2,1,0:T(4,128)(2,1)}), bf16[64,3,2048]{2,1,0:T(4,128)(2,1)}, u32[]{:S(2)}, u32[]{:S(2)}) %all-to-all-start.8) | async-done | bytes 786464 | tf_op jit(solution)/shard_map/all_to_all | solution.py:52
  350.9 26.9 %all-to-all-done.10 = bf16[64,3,2048]{2,1,0:T(4,128)(2,1)} async-done(((bf16[64,3,2048]{2,1,0:T(4,128)(2,1)}), bf16[64,3,2048]{2,1,0:T(4,128)(2,1)}, u32[]{:S(2)}, u32[]{:S(2)}) %all-to-all-start.10) | async-done | bytes 786464 | tf_op jit(solution)/shard_map/all_to_all | solution.py:45
  399.7 21.5 %all-to-all-done.11 = bf16[64,3,2048]{2,1,0:T(4,128)(2,1)} async-done(((bf16[64,3,2048]{2,1,0:T(4,128)(2,1)}), bf16[64,3,2048]{2,1,0:T(4,128)(2,1)}, u32[]{:S(2)}, u32[]{:S(2)}) %all-to-all-start.11) | async-done | bytes 786464 | tf_op jit(solution)/shard_map/all_to_all | solution.py:52
  452.8 21.8 %all-to-all-done.13 = bf16[64,3,2048]{2,1,0:T(4,128)(2,1)} async-done(((bf16[64,3,2048]{2,1,0:T(4,128)(2,1)}), bf16[64,3,2048]{2,1,0:T(4,128)(2,1)}, u32[]{:S(2)}, u32[]{:S(2)}) %all-to-all-start.13) | async-done | bytes 786464 | tf_op jit(solution)/shard_map/all_to_all | solution.py:45
  486.5 24.1 %all-to-all-done.14 = bf16[64,3,2048]{2,1,0:T(4,128)(2,1)} async-done(((bf16[64,3,2048]{2,1,0:T(4,128)(2,1)}), bf16[64,3,2048]{2,1,0:T(4,128)(2,1)}, u32[]{:S(2)}, u32[]{:S(2)}) %all-to-all-start.14) | async-done | bytes 786464 | tf_op jit(solution)/shard_map/all_to_all | solution.py:52
  542.1 22.4 %all-to-all-done.16 = bf16[64,3,2048]{2,1,0:T(4,128)(2,1)} async-done(((bf16[64,3,2048]{2,1,0:T(4,128)(2,1)}), bf16[64,3,2048]{2,1,0:T(4,128)(2,1)}, u32[]{:S(2)}, u32[]{:S(2)}) %all-to-all-start.16) | async-done | bytes 786464 | tf_op jit(solution)/shard_map/all_to_all | solution.py:45
  580.6 26.7 %all-to-all-done.17 = bf16[64,3,2048]{2,1,0:T(4,128)(2,1)} async-done(((bf16[64,3,2048]{2,1,0:T(4,128)(2,1)}), bf16[64,3,2048]{2,1,0:T(4,128)(2,1)}, u32[]{:S(2)}, u32[]{:S(2)}) %all-to-all-start.17) | async-done | bytes 786464 | tf_op jit(solution)/shard_map/all_to_all | solution.py:52
  642.5 23.4 %all-to-all-done.19 = bf16[64,3,2048]{2,1,0:T(4,128)(2,1)} async-done(((bf16[64,3,2048]{2,1,0:T(4,128)(2,1)}), bf16[64,3,2048]{2,1,0:T(4,128)(2,1)}, u32[]{:S(2)}, u32[]{:S(2)}) %all-to-all-start.19) | async-done | bytes 786464 | tf_op jit(solution)/shard_map/all_to_all | solution.py:45
  701.7 20.6 %all-to-all-done.22 = bf16[64,3,2048]{2,1,0:T(4,128)(2,1)} async-done(((bf16[64,3,2048]{2,1,0:T(4,128)(2,1)}), bf16[64,3,2048]{2,1,0:T(4,128)(2,1)}, u32[]{:S(2)}, u32[]{:S(2)}) %all-to-all-start.22) | async-done | bytes 786464 | tf_op jit(solution)/shard_map/all_to_all | solution.py:60
  750.4 28.5 %all-to-all-done.23 = bf16[64,3,2048]{2,1,0:T(4,128)(2,1)} async-done(((bf16[64,3,2048]{2,1,0:T(4,128)(2,1)}), bf16[64,3,2048]{2,1,0:T(4,128)(2,1)}, u32[]{:S(2)}, u32[]{:S(2)}) %all-to-all-start.23) | async-done | bytes 786464 | tf_op jit(solution)/shard_map/all_to_all | solution.py:56
  788.4 19.0 %all-to-all-done.24 = bf16[64,3,2048]{2,1,0:T(4,128)(2,1)} async-done(((bf16[64,3,2048]{2,1,0:T(4,128)(2,1)}), bf16[64,3,2048]{2,1,0:T(4,128)(2,1)}, u32[]{:S(2)}, u32[]{:S(2)}) %all-to-all-start.24) | async-done | bytes 786464 | tf_op jit(solution)/shard_map/all_to_all | solution.py:60
  839.6 28.5 %all-to-all-done.25 = bf16[64,3,2048]{2,1,0:T(4,128)(2,1)} async-done(((bf16[64,3,2048]{2,1,0:T(4,128)(2,1)}), bf16[64,3,2048]{2,1,0:T(4,128)(2,1)}, u32[]{:S(2)}, u32[]{:S(2)}) %all-to-all-start.25) | async-done | bytes 786464 | tf_op jit(solution)/shard_map/all_to_all | solution.py:56
  877.8 19.0 %all-to-all-done.26 = bf16[64,3,2048]{2,1,0:T(4,128)(2,1)} async-done(((bf16[64,3,2048]{2,1,0:T(4,128)(2,1)}), bf16[64,3,2048]{2,1,0:T(4,128)(2,1)}, u32[]{:S(2)}, u32[]{:S(2)}) %all-to-all-start.26) | async-done | bytes 786464 | tf_op jit(solution)/shard_map/all_to_all | solution.py:60
  930.2 28.5 %all-to-all-done.27 = bf16[64,3,2048]{2,1,0:T(4,128)(2,1)} async-done(((bf16[64,3,2048]{2,1,0:T(4,128)(2,1)}), bf16[64,3,2048]{2,1,0:T(4,128)(2,1)}, u32[]{:S(2)}, u32[]{:S(2)}) %all-to-all-start.27) | async-done | bytes 786464 | tf_op jit(solution)/shard_map/all_to_all | solution.py:56
  976.9 19.1 %all-to-all-done.28 = bf16[64,3,2048]{2,1,0:T(4,128)(2,1)} async-done(((bf16[64,3,2048]{2,1,0:T(4,128)(2,1)}), bf16[64,3,2048]{2,1,0:T(4,128)(2,1)}, u32[]{:S(2)}, u32[]{:S(2)}) %all-to-all-start.28) | async-done | bytes 786464 | tf_op jit(solution)/shard_map/all_to_all | solution.py:60
  1020.2 28.5 %all-to-all-done.29 = bf16[64,3,2048]{2,1,0:T(4,128)(2,1)} async-done(((bf16[64,3,2048]{2,1,0:T(4,128)(2,1)}), bf16[64,3,2048]{2,1,0:T(4,128)(2,1)}, u32[]{:S(2)}, u32[]{:S(2)}) %all-to-all-start.29) | async-done | bytes 786464 | tf_op jit(solution)/shard_map/all_to_all | solution.py:56
  1066.9 19.1 %all-to-all-done.30 = bf16[64,3,2048]{2,1,0:T(4,128)(2,1)} async-done(((bf16[64,3,2048]{2,1,0:T(4,128)(2,1)}), bf16[64,3,2048]{2,1,0:T(4,128)(2,1)}, u32[]{:S(2)}, u32[]{:S(2)}) %all-to-all-start.30) | async-done | bytes 786464 | tf_op jit(solution)/shard_map/all_to_all | solution.py:60
  1091.4 23.4 %collective-permute-done.10 = bf16[32,2048]{1,0:T(8,128)(2,1)S(1)} collective-permute-done((bf16[32,2048]{1,0:T(8,128)(2,1)S(1)}, bf16[32,2048]{1,0:T(8,128)(2,1)S(1)}, u32[]{:S(2)}, u32[]{:S(2)}) %collective-permute-start.10) | collective-permute-done | bytes 131104 | tf_op jit(solution)/shard_map/ppermute | solution.py:13
  1123.6 28.0 %all-to-all-done.31 = bf16[64,3,2048]{2,1,0:T(4,128)(2,1)} async-done(((bf16[64,3,2048]{2,1,0:T(4,128)(2,1)}), bf16[64,3,2048]{2,1,0:T(4,128)(2,1)}, u32[]{:S(2)}, u32[]{:S(2)}) %all-to-all-start.31) | async-done | bytes 786464 | tf_op jit(solution)/shard_map/all_to_all | solution.py:56
  1170.2 27.8 %all-to-all-done.32 = bf16[64,3,2048]{2,1,0:T(4,128)(2,1)} async-done(((bf16[64,3,2048]{2,1,0:T(4,128)(2,1)}), bf16[64,3,2048]{2,1,0:T(4,128)(2,1)}, u32[]{:S(2)}, u32[]{:S(2)}) %all-to-all-start.32) | async-done | bytes 786464 | tf_op jit(solution)/shard_map/all_to_all | solution.py:60
  1302.3 203.1 %psum.7 = f32[1,2048]{1,0:T(1,128)} all-reduce(f32[1,2048]{1,0:T(1,128)S(1)} %bitcast.633), channel_id=1, replica_groups=mesh['dp'=8,'pipe'=4,'expert'=8] {'dp','expert'}, use_global_device_ids=true, to_apply=%region_84.85 | all-reduce | flops 2048 | bytes 16384 | tf_op jit(solution)/shard_map/psum | solution.py:226
  (416 shorter events, 826.0 us)
Async XLA Ops:
  5.5 27.2 %all-to-all-start = ((bf16[64,3,1]{1,2,0:T(2,128)(2,1)}), bf16[64,3,1]{1,2,0:T(2,128)(2,1)S(1)}, u32[]{:S(2)}, u32[]{:S(2)}) async-start(bf16[64,3,1]{1,2,0:T(2,128)(2,1)} %copy.214), calls=%async_computation | async-start | bytes 65536 | tf_op jit(solution)/shard_map/all_to_all | solution.py:46
  32.7 33.2 %all-to-all-start.1 = ((bf16[64,3,2048]{2,1,0:T(4,128)(2,1)}), bf16[64,3,2048]{2,1,0:T(4,128)(2,1)}, u32[]{:S(2)}, u32[]{:S(2)}) async-start(bf16[64,3,2048]{2,1,0:T(4,128)(2,1)} %copy.215), calls=%async_computation.1 | async-start | bytes 2097152 | tf_op jit(solution)/shard_map/all_to_all | solution.py:45
  78.3 24.5 %all-to-all-start.2 = ((bf16[64,3,2048]{2,1,0:T(4,128)(2,1)}), bf16[64,3,2048]{2,1,0:T(4,128)(2,1)}, u32[]{:S(2)}, u32[]{:S(2)}) async-start(bf16[64,3,2048]{2,1,0:T(4,128)(2,1)} %reshape.639), calls=%async_computation.2 | async-start | bytes 2097152 | tf_op jit(solution)/shard_map/all_to_all | solution.py:52
  122.4 43.0 %all-to-all-start.4 = ((bf16[64,3,2048]{2,1,0:T(4,128)(2,1)}), bf16[64,3,2048]{2,1,0:T(4,128)(2,1)}, u32[]{:S(2)}, u32[]{:S(2)}) async-start(bf16[64,3,2048]{2,1,0:T(4,128)(2,1)} %copy.219), calls=%async_computation.4 | async-start | bytes 2097152 | tf_op jit(solution)/shard_map/all_to_all | solution.py:45
  240.8 34.5 %all-to-all-start.7 = ((bf16[64,3,2048]{2,1,0:T(4,128)(2,1)}), bf16[64,3,2048]{2,1,0:T(4,128)(2,1)}, u32[]{:S(2)}, u32[]{:S(2)}) async-start(bf16[64,3,2048]{2,1,0:T(4,128)(2,1)} %copy.223), calls=%async_computation.7 | async-start | bytes 2097152 | tf_op jit(solution)/shard_map/all_to_all | solution.py:45
  287.7 31.1 %all-to-all-start.8 = ((bf16[64,3,2048]{2,1,0:T(4,128)(2,1)}), bf16[64,3,2048]{2,1,0:T(4,128)(2,1)}, u32[]{:S(2)}, u32[]{:S(2)}) async-start(bf16[64,3,2048]{2,1,0:T(4,128)(2,1)} %reshape.643), calls=%async_computation.8 | async-start | bytes 2097152 | tf_op jit(solution)/shard_map/all_to_all | solution.py:52
  345.1 32.7 %all-to-all-start.10 = ((bf16[64,3,2048]{2,1,0:T(4,128)(2,1)}), bf16[64,3,2048]{2,1,0:T(4,128)(2,1)}, u32[]{:S(2)}, u32[]{:S(2)}) async-start(bf16[64,3,2048]{2,1,0:T(4,128)(2,1)} %copy.227), calls=%async_computation.10 | async-start | bytes 2097152 | tf_op jit(solution)/shard_map/all_to_all | solution.py:45
  390.2 31.1 %all-to-all-start.11 = ((bf16[64,3,2048]{2,1,0:T(4,128)(2,1)}), bf16[64,3,2048]{2,1,0:T(4,128)(2,1)}, u32[]{:S(2)}, u32[]{:S(2)}) async-start(bf16[64,3,2048]{2,1,0:T(4,128)(2,1)} %reshape.645), calls=%async_computation.11 | async-start | bytes 2097152 | tf_op jit(solution)/shard_map/all_to_all | solution.py:52
  447.0 27.6 %all-to-all-start.13 = ((bf16[64,3,2048]{2,1,0:T(4,128)(2,1)}), bf16[64,3,2048]{2,1,0:T(4,128)(2,1)}, u32[]{:S(2)}, u32[]{:S(2)}) async-start(bf16[64,3,2048]{2,1,0:T(4,128)(2,1)} %copy.231), calls=%async_computation.13 | async-start | bytes 2097152 | tf_op jit(solution)/shard_map/all_to_all | solution.py:45
  479.9 30.7 %all-to-all-start.14 = ((bf16[64,3,2048]{2,1,0:T(4,128)(2,1)}), bf16[64,3,2048]{2,1,0:T(4,128)(2,1)}, u32[]{:S(2)}, u32[]{:S(2)}) async-start(bf16[64,3,2048]{2,1,0:T(4,128)(2,1)} %reshape.647), calls=%async_computation.14 | async-start | bytes 2097152 | tf_op jit(solution)/shard_map/all_to_all | solution.py:52
  536.3 28.2 %all-to-all-start.16 = ((bf16[64,3,2048]{2,1,0:T(4,128)(2,1)}), bf16[64,3,2048]{2,1,0:T(4,128)(2,1)}, u32[]{:S(2)}, u32[]{:S(2)}) async-start(bf16[64,3,2048]{2,1,0:T(4,128)(2,1)} %copy.235), calls=%async_computation.16 | async-start | bytes 2097152 | tf_op jit(solution)/shard_map/all_to_all | solution.py:45
  569.6 37.7 %all-to-all-start.17 = ((bf16[64,3,2048]{2,1,0:T(4,128)(2,1)}), bf16[64,3,2048]{2,1,0:T(4,128)(2,1)}, u32[]{:S(2)}, u32[]{:S(2)}) async-start(bf16[64,3,2048]{2,1,0:T(4,128)(2,1)} %reshape.649), calls=%async_computation.17 | async-start | bytes 2097152 | tf_op jit(solution)/shard_map/all_to_all | solution.py:52
  631.6 34.4 %all-to-all-start.19 = ((bf16[64,3,2048]{2,1,0:T(4,128)(2,1)}), bf16[64,3,2048]{2,1,0:T(4,128)(2,1)}, u32[]{:S(2)}, u32[]{:S(2)}) async-start(bf16[64,3,2048]{2,1,0:T(4,128)(2,1)} %copy.239), calls=%async_computation.19 | async-start | bytes 2097152 | tf_op jit(solution)/shard_map/all_to_all | solution.py:45
  694.6 27.6 %all-to-all-start.22 = ((bf16[64,3,2048]{2,1,0:T(4,128)(2,1)}), bf16[64,3,2048]{2,1,0:T(4,128)(2,1)}, u32[]{:S(2)}, u32[]{:S(2)}) async-start(bf16[64,3,2048]{2,1,0:T(4,128)(2,1)} %reshape.654), calls=%async_computation.22 | async-start | bytes 2097152 | tf_op jit(solution)/shard_map/all_to_all | solution.py:60
  744.6 34.2 %all-to-all-start.23 = ((bf16[64,3,2048]{2,1,0:T(4,128)(2,1)}), bf16[64,3,2048]{2,1,0:T(4,128)(2,1)}, u32[]{:S(2)}, u32[]{:S(2)}) async-start(bf16[64,3,2048]{2,1,0:T(4,128)(2,1)} %copy.251), calls=%async_computation.23 | async-start | bytes 2097152 | tf_op jit(solution)/shard_map/all_to_all | solution.py:56
  827.4 40.7 %all-to-all-start.25 = ((bf16[64,3,2048]{2,1,0:T(4,128)(2,1)}), bf16[64,3,2048]{2,1,0:T(4,128)(2,1)}, u32[]{:S(2)}, u32[]{:S(2)}) async-start(bf16[64,3,2048]{2,1,0:T(4,128)(2,1)} %copy.253), calls=%async_computation.25 | async-start | bytes 2097152 | tf_op jit(solution)/shard_map/all_to_all | solution.py:56
  922.4 36.3 %all-to-all-start.27 = ((bf16[64,3,2048]{2,1,0:T(4,128)(2,1)}), bf16[64,3,2048]{2,1,0:T(4,128)(2,1)}, u32[]{:S(2)}, u32[]{:S(2)}) async-start(bf16[64,3,2048]{2,1,0:T(4,128)(2,1)} %copy.255), calls=%async_computation.27 | async-start | bytes 2097152 | tf_op jit(solution)/shard_map/all_to_all | solution.py:56
  1012.4 36.3 %all-to-all-start.29 = ((bf16[64,3,2048]{2,1,0:T(4,128)(2,1)}), bf16[64,3,2048]{2,1,0:T(4,128)(2,1)}, u32[]{:S(2)}, u32[]{:S(2)}) async-start(bf16[64,3,2048]{2,1,0:T(4,128)(2,1)} %copy.257), calls=%async_computation.29 | async-start | bytes 2097152 | tf_op jit(solution)/shard_map/all_to_all | solution.py:56
  1090.1 24.7 %collective-permute-start.10 = (bf16[32,2048]{1,0:T(8,128)(2,1)S(1)}, bf16[32,2048]{1,0:T(8,128)(2,1)S(1)}, u32[]{:S(2)}, u32[]{:S(2)}) collective-permute-start(bf16[32,2048]{1,0:T(8,128)(2,1)S(1)} %get-tuple-element.782), channel_id=1, source_target_pairs={{8,0},{16,8},{24,16},{9,1},{17,9},{25,17},{10,2},{18,10},{26,18},{... | collective-permute-start | bytes 393224 | tf_op jit(solution)/shard_map/ppermute | solution.py:13
  1117.9 33.7 %all-to-all-start.31 = ((bf16[64,3,2048]{2,1,0:T(4,128)(2,1)}), bf16[64,3,2048]{2,1,0:T(4,128)(2,1)}, u32[]{:S(2)}, u32[]{:S(2)}) async-start(bf16[64,3,2048]{2,1,0:T(4,128)(2,1)} %copy.259), calls=%async_computation.31 | async-start | bytes 2097152 | tf_op jit(solution)/shard_map/all_to_all | solution.py:56
  1164.6 33.5 %all-to-all-start.32 = ((bf16[64,3,2048]{2,1,0:T(4,128)(2,1)}), bf16[64,3,2048]{2,1,0:T(4,128)(2,1)}, u32[]{:S(2)}, u32[]{:S(2)}) async-start(bf16[64,3,2048]{2,1,0:T(4,128)(2,1)} %reshape.664), calls=%async_computation.32 | async-start | bytes 2097152 | tf_op jit(solution)/shard_map/all_to_all | solution.py:60
  1211.5 31.9 %all-to-all-start.33 = ((bf16[64,3,2048]{2,1,0:T(4,128)(2,1)}), bf16[64,3,2048]{2,1,0:T(4,128)(2,1)}, u32[]{:S(2)}, u32[]{:S(2)}) async-start(bf16[64,3,2048]{2,1,0:T(4,128)(2,1)} %copy.261), calls=%async_computation.33 | async-start | bytes 2097152 | tf_op jit(solution)/shard_map/all_to_all | solution.py:56
  1243.3 29.7 %all-to-all-start.20 = ((bf16[64,3,2048]{2,1,0:T(4,128)(2,1)}), bf16[64,3,2048]{2,1,0:T(4,128)(2,1)}, u32[]{:S(2)}, u32[]{:S(2)}) async-start(bf16[64,3,2048]{2,1,0:T(4,128)(2,1)} %reshape.651), calls=%async_computation.20 | async-start | bytes 2097152 | tf_op jit(solution)/shard_map/all_to_all | solution.py:52
  1273.1 27.2 %all-to-all-start.34 = ((bf16[64,3,2048]{2,1,0:T(4,128)(2,1)}), bf16[64,3,2048]{2,1,0:T(4,128)(2,1)S(1)}, u32[]{:S(2)}, u32[]{:S(2)}) async-start(bf16[64,3,2048]{2,1,0:T(4,128)(2,1)} %reshape.666), calls=%async_computation.34 | async-start | bytes 2097152 | tf_op jit(solution)/shard_map/all_to_all | solution.py:60
  (51 other events, 836.2 us)
where the time goes:
time: 1520 us; the launch traced here: 1510 us
  waiting for transfers between devices  747 us (49%)
  starting transfers between devices  290 us (19%)
  blocking collectives  203 us (13%)
  local copies, waits for them, and re-layouts  141 us (9%)
  matrix products  92.5 us (6%)
  other arithmetic  31.6 us (2%)
    psum x1, blocking collectives, body(): gain_grad = lax.psum(gain_sum, ('dp', 'expert'))  203 us
    all_to_all x7, waiting for transfers between devices, send_rows(): lax.all_to_all(row_block, ('dp', 'expert'), split_axis=0, concat_axis=0,...  177 us
    all_to_all x7, waiting for transfers between devices, send_grads(): lax.all_to_all(row_block, ('dp', 'expert'), split_axis=0, concat_axis=0,...  165 us
    all_to_all x7, waiting for transfers between devices, return_grads(): lax.all_to_all(row_block, ('dp', 'expert'), split_axis=0, concat_axis=0,...  144 us
    all_to_all x7, waiting for transfers between devices, return_rows(): lax.all_to_all(row_block, ('dp', 'expert'), split_axis=0, concat_axis=0,...  138 us
    ppermute x12, waiting for transfers between devices, from_behind(): lax.ppermute(value, axis, [(source, source + steps) for source in range(l...  79.9 us
    all_to_all x7, starting transfers between devices, send_rows(): lax.all_to_all(pair_block, ('dp', 'expert'), split_axis=0, concat_axis=0,...  58 us
    all_to_all x7, starting transfers between devices, send_grads(): lax.all_to_all(row_block, ('dp', 'expert'), split_axis=0, concat_axis=0,...  54.3 us
  transfers between devices with their start and end apart: 47, of which 41 were waited for; matrix products, arithmetic and copies ran while one was open for 5% of the time, Pallas kernels for 0%

commit v1 on v0

--- a/solution.py
+++ b/solution.py
@@ -223,7 +223,7 @@
         gain_sum = gain_sum + gain_term
         if tick_num + 1 < ticks:
             incoming = from_behind(grad_bf, "pipe", -1)
-    gain_grad = lax.psum(gain_sum, ("dp", "expert"))
+    gain_grad = lax.psum(lax.psum(gain_sum, "expert"), "dp")
     segment_out = layer_outs[:MICRO].reshape(1, tok_rows, width)
     segment_grad = grad_outs[:MICRO].reshape(1, tok_rows, width)
     return (segment_out, segment_grad, gain_grad.reshape(1, width))

time: 1520 us -> 1360 us (0.89)
  blocking collectives: 203 us -> 35 us
    psum x1 -> x2, blocking collectives: 203 us -> 35 us  [body(): gain_grad = lax.psum(lax.psum(gain_sum, 'expert'), 'dp')]
  transfers between devices with their start and end apart: 47 -> 47, of which waited for: 41 -> 41; matrix products, arithmetic and copies ran while one was open for 5% -> 6% of each run, Pallas kernels for 0% -> 0%
where the time goes in v1:
time: 1360 us; the launch traced here: 1340 us
  waiting for transfers between devices  747 us (55%)
  starting transfers between devices  290 us (21%)
  local copies, waits for them, and re-layouts  141 us (10%)
  matrix products  92.5 us (7%)
  blocking collectives  35 us (3%)
  other arithmetic  31.6 us (2%)
    all_to_all x7, waiting for transfers between devices, send_rows(): lax.all_to_all(row_block, ('dp', 'expert'), split_axis=0, concat_axis=0,...  177 us
    all_to_all x7, waiting for transfers between devices, send_grads(): lax.all_to_all(row_block, ('dp', 'expert'), split_axis=0, concat_axis=0,...  165 us
    all_to_all x7, waiting for transfers between devices, return_grads(): lax.all_to_all(row_block, ('dp', 'expert'), split_axis=0, concat_axis=0,...  143 us
    all_to_all x7, waiting for transfers between devices, return_rows(): lax.all_to_all(row_block, ('dp', 'expert'), split_axis=0, concat_axis=0,...  138 us
    ppermute x12, waiting for transfers between devices, from_behind(): lax.ppermute(value, axis, [(source, source + steps) for source in range(l...  79.9 us
    all_to_all x7, starting transfers between devices, send_rows(): lax.all_to_all(pair_block, ('dp', 'expert'), split_axis=0, concat_axis=0,...  58 us
    all_to_all x7, starting transfers between devices, send_grads(): lax.all_to_all(row_block, ('dp', 'expert'), split_axis=0, concat_axis=0,...  54.3 us
    all_to_all x7, starting transfers between devices, return_rows(): lax.all_to_all(row_block, ('dp', 'expert'), split_axis=0, concat_axis=0,...  50.9 us
  transfers between devices with their start and end apart: 47, of which 41 were waited for; matrix products, arithmetic and copies ran while one was open for 6% of the time, Pallas kernels for 0%

profile of v1, /device:TPU:1, one launch (start us, length us, event | category | flops | bytes accessed | tf_op | source)
XLA Modules:
  0.0 1339.5 jit_solution(3824412371757008780)
XLA Ops:
  40.4 25.5 %all-to-all-done.1 = bf16[64,3,2048]{2,1,0:T(4,128)(2,1)} async-done(((bf16[64,3,2048]{2,1,0:T(4,128)(2,1)}), bf16[64,3,2048]{2,1,0:T(4,128)(2,1)}, u32[]{:S(2)}, u32[]{:S(2)}) %all-to-all-start.1) | async-done | bytes 786464 | tf_op jit(solution)/shard_map/all_to_all | solution.py:45
  136.9 28.5 %all-to-all-done.4 = bf16[64,3,2048]{2,1,0:T(4,128)(2,1)} async-done(((bf16[64,3,2048]{2,1,0:T(4,128)(2,1)}), bf16[64,3,2048]{2,1,0:T(4,128)(2,1)}, u32[]{:S(2)}, u32[]{:S(2)}) %all-to-all-start.4) | async-done | bytes 786464 | tf_op jit(solution)/shard_map/all_to_all | solution.py:45
  246.7 28.6 %all-to-all-done.7 = bf16[64,3,2048]{2,1,0:T(4,128)(2,1)} async-done(((bf16[64,3,2048]{2,1,0:T(4,128)(2,1)}), bf16[64,3,2048]{2,1,0:T(4,128)(2,1)}, u32[]{:S(2)}, u32[]{:S(2)}) %all-to-all-start.7) | async-done | bytes 786464 | tf_op jit(solution)/shard_map/all_to_all | solution.py:45
  298.6 20.2 %all-to-all-done.8 = bf16[64,3,2048]{2,1,0:T(4,128)(2,1)} async-done(((bf16[64,3,2048]{2,1,0:T(4,128)(2,1)}), bf16[64,3,2048]{2,1,0:T(4,128)(2,1)}, u32[]{:S(2)}, u32[]{:S(2)}) %all-to-all-start.8) | async-done | bytes 786464 | tf_op jit(solution)/shard_map/all_to_all | solution.py:52
  350.9 26.9 %all-to-all-done.10 = bf16[64,3,2048]{2,1,0:T(4,128)(2,1)} async-done(((bf16[64,3,2048]{2,1,0:T(4,128)(2,1)}), bf16[64,3,2048]{2,1,0:T(4,128)(2,1)}, u32[]{:S(2)}, u32[]{:S(2)}) %all-to-all-start.10) | async-done | bytes 786464 | tf_op jit(solution)/shard_map/all_to_all | solution.py:45
  399.7 21.5 %all-to-all-done.11 = bf16[64,3,2048]{2,1,0:T(4,128)(2,1)} async-done(((bf16[64,3,2048]{2,1,0:T(4,128)(2,1)}), bf16[64,3,2048]{2,1,0:T(4,128)(2,1)}, u32[]{:S(2)}, u32[]{:S(2)}) %all-to-all-start.11) | async-done | bytes 786464 | tf_op jit(solution)/shard_map/all_to_all | solution.py:52
  452.8 21.8 %all-to-all-done.13 = bf16[64,3,2048]{2,1,0:T(4,128)(2,1)} async-done(((bf16[64,3,2048]{2,1,0:T(4,128)(2,1)}), bf16[64,3,2048]{2,1,0:T(4,128)(2,1)}, u32[]{:S(2)}, u32[]{:S(2)}) %all-to-all-start.13) | async-done | bytes 786464 | tf_op jit(solution)/shard_map/all_to_all | solution.py:45
  486.5 24.1 %all-to-all-done.14 = bf16[64,3,2048]{2,1,0:T(4,128)(2,1)} async-done(((bf16[64,3,2048]{2,1,0:T(4,128)(2,1)}), bf16[64,3,2048]{2,1,0:T(4,128)(2,1)}, u32[]{:S(2)}, u32[]{:S(2)}) %all-to-all-start.14) | async-done | bytes 786464 | tf_op jit(solution)/shard_map/all_to_all | solution.py:52
  542.1 22.4 %all-to-all-done.16 = bf16[64,3,2048]{2,1,0:T(4,128)(2,1)} async-done(((bf16[64,3,2048]{2,1,0:T(4,128)(2,1)}), bf16[64,3,2048]{2,1,0:T(4,128)(2,1)}, u32[]{:S(2)}, u32[]{:S(2)}) %all-to-all-start.16) | async-done | bytes 786464 | tf_op jit(solution)/shard_map/all_to_all | solution.py:45
  580.6 26.7 %all-to-all-done.17 = bf16[64,3,2048]{2,1,0:T(4,128)(2,1)} async-done(((bf16[64,3,2048]{2,1,0:T(4,128)(2,1)}), bf16[64,3,2048]{2,1,0:T(4,128)(2,1)}, u32[]{:S(2)}, u32[]{:S(2)}) %all-to-all-start.17) | async-done | bytes 786464 | tf_op jit(solution)/shard_map/all_to_all | solution.py:52
  642.5 23.4 %all-to-all-done.19 = bf16[64,3,2048]{2,1,0:T(4,128)(2,1)} async-done(((bf16[64,3,2048]{2,1,0:T(4,128)(2,1)}), bf16[64,3,2048]{2,1,0:T(4,128)(2,1)}, u32[]{:S(2)}, u32[]{:S(2)}) %all-to-all-start.19) | async-done | bytes 786464 | tf_op jit(solution)/shard_map/all_to_all | solution.py:45
  701.7 20.6 %all-to-all-done.22 = bf16[64,3,2048]{2,1,0:T(4,128)(2,1)} async-done(((bf16[64,3,2048]{2,1,0:T(4,128)(2,1)}), bf16[64,3,2048]{2,1,0:T(4,128)(2,1)}, u32[]{:S(2)}, u32[]{:S(2)}) %all-to-all-start.22) | async-done | bytes 786464 | tf_op jit(solution)/shard_map/all_to_all | solution.py:60
  750.4 28.5 %all-to-all-done.23 = bf16[64,3,2048]{2,1,0:T(4,128)(2,1)} async-done(((bf16[64,3,2048]{2,1,0:T(4,128)(2,1)}), bf16[64,3,2048]{2,1,0:T(4,128)(2,1)}, u32[]{:S(2)}, u32[]{:S(2)}) %all-to-all-start.23) | async-done | bytes 786464 | tf_op jit(solution)/shard_map/all_to_all | solution.py:56
  788.4 19.0 %all-to-all-done.24 = bf16[64,3,2048]{2,1,0:T(4,128)(2,1)} async-done(((bf16[64,3,2048]{2,1,0:T(4,128)(2,1)}), bf16[64,3,2048]{2,1,0:T(4,128)(2,1)}, u32[]{:S(2)}, u32[]{:S(2)}) %all-to-all-start.24) | async-done | bytes 786464 | tf_op jit(solution)/shard_map/all_to_all | solution.py:60
  839.6 28.5 %all-to-all-done.25 = bf16[64,3,2048]{2,1,0:T(4,128)(2,1)} async-done(((bf16[64,3,2048]{2,1,0:T(4,128)(2,1)}), bf16[64,3,2048]{2,1,0:T(4,128)(2,1)}, u32[]{:S(2)}, u32[]{:S(2)}) %all-to-all-start.25) | async-done | bytes 786464 | tf_op jit(solution)/shard_map/all_to_all | solution.py:56
  877.8 19.0 %all-to-all-done.26 = bf16[64,3,2048]{2,1,0:T(4,128)(2,1)} async-done(((bf16[64,3,2048]{2,1,0:T(4,128)(2,1)}), bf16[64,3,2048]{2,1,0:T(4,128)(2,1)}, u32[]{:S(2)}, u32[]{:S(2)}) %all-to-all-start.26) | async-done | bytes 786464 | tf_op jit(solution)/shard_map/all_to_all | solution.py:60
  930.2 28.5 %all-to-all-done.27 = bf16[64,3,2048]{2,1,0:T(4,128)(2,1)} async-done(((bf16[64,3,2048]{2,1,0:T(4,128)(2,1)}), bf16[64,3,2048]{2,1,0:T(4,128)(2,1)}, u32[]{:S(2)}, u32[]{:S(2)}) %all-to-all-start.27) | async-done | bytes 786464 | tf_op jit(solution)/shard_map/all_to_all | solution.py:56
  976.9 19.1 %all-to-all-done.28 = bf16[64,3,2048]{2,1,0:T(4,128)(2,1)} async-done(((bf16[64,3,2048]{2,1,0:T(4,128)(2,1)}), bf16[64,3,2048]{2,1,0:T(4,128)(2,1)}, u32[]{:S(2)}, u32[]{:S(2)}) %all-to-all-start.28) | async-done | bytes 786464 | tf_op jit(solution)/shard_map/all_to_all | solution.py:60
  1020.2 28.5 %all-to-all-done.29 = bf16[64,3,2048]{2,1,0:T(4,128)(2,1)} async-done(((bf16[64,3,2048]{2,1,0:T(4,128)(2,1)}), bf16[64,3,2048]{2,1,0:T(4,128)(2,1)}, u32[]{:S(2)}, u32[]{:S(2)}) %all-to-all-start.29) | async-done | bytes 786464 | tf_op jit(solution)/shard_map/all_to_all | solution.py:56
  1066.9 19.1 %all-to-all-done.30 = bf16[64,3,2048]{2,1,0:T(4,128)(2,1)} async-done(((bf16[64,3,2048]{2,1,0:T(4,128)(2,1)}), bf16[64,3,2048]{2,1,0:T(4,128)(2,1)}, u32[]{:S(2)}, u32[]{:S(2)}) %all-to-all-start.30) | async-done | bytes 786464 | tf_op jit(solution)/shard_map/all_to_all | solution.py:60
  1091.4 23.4 %collective-permute-done.10 = bf16[32,2048]{1,0:T(8,128)(2,1)S(1)} collective-permute-done((bf16[32,2048]{1,0:T(8,128)(2,1)S(1)}, bf16[32,2048]{1,0:T(8,128)(2,1)S(1)}, u32[]{:S(2)}, u32[]{:S(2)}) %collective-permute-start.10) | collective-permute-done | bytes 131104 | tf_op jit(solution)/shard_map/ppermute | solution.py:13
  1123.6 28.0 %all-to-all-done.31 = bf16[64,3,2048]{2,1,0:T(4,128)(2,1)} async-done(((bf16[64,3,2048]{2,1,0:T(4,128)(2,1)}), bf16[64,3,2048]{2,1,0:T(4,128)(2,1)}, u32[]{:S(2)}, u32[]{:S(2)}) %all-to-all-start.31) | async-done | bytes 786464 | tf_op jit(solution)/shard_map/all_to_all | solution.py:56
  1170.2 27.8 %all-to-all-done.32 = bf16[64,3,2048]{2,1,0:T(4,128)(2,1)} async-done(((bf16[64,3,2048]{2,1,0:T(4,128)(2,1)}), bf16[64,3,2048]{2,1,0:T(4,128)(2,1)}, u32[]{:S(2)}, u32[]{:S(2)}) %all-to-all-start.32) | async-done | bytes 786464 | tf_op jit(solution)/shard_map/all_to_all | solution.py:60
  1314.5 22.7 %psum.15 = f32[1,2048]{1,0:T(1,128)} all-reduce(f32[1,2048]{1,0:T(1,128)S(1)} %bitcast.633), channel_id=1, replica_groups=mesh['dp'=8,'pipe'=4,'expert'=8] {'dp'}, use_global_device_ids=true, to_apply=%region_85.86 | all-reduce | flops 2048 | bytes 16384 | tf_op jit(solution)/shard_map/psum | solution.py:226
  (417 shorter events, 838.1 us)
Async XLA Ops:
  5.5 27.2 %all-to-all-start = ((bf16[64,3,1]{1,2,0:T(2,128)(2,1)}), bf16[64,3,1]{1,2,0:T(2,128)(2,1)S(1)}, u32[]{:S(2)}, u32[]{:S(2)}) async-start(bf16[64,3,1]{1,2,0:T(2,128)(2,1)} %copy.214), calls=%async_computation | async-start | bytes 65536 | tf_op jit(solution)/shard_map/all_to_all | solution.py:46
  32.7 33.2 %all-to-all-start.1 = ((bf16[64,3,2048]{2,1,0:T(4,128)(2,1)}), bf16[64,3,2048]{2,1,0:T(4,128)(2,1)}, u32[]{:S(2)}, u32[]{:S(2)}) async-start(bf16[64,3,2048]{2,1,0:T(4,128)(2,1)} %copy.215), calls=%async_computation.1 | async-start | bytes 2097152 | tf_op jit(solution)/shard_map/all_to_all | solution.py:45
  78.3 24.5 %all-to-all-start.2 = ((bf16[64,3,2048]{2,1,0:T(4,128)(2,1)}), bf16[64,3,2048]{2,1,0:T(4,128)(2,1)}, u32[]{:S(2)}, u32[]{:S(2)}) async-start(bf16[64,3,2048]{2,1,0:T(4,128)(2,1)} %reshape.639), calls=%async_computation.2 | async-start | bytes 2097152 | tf_op jit(solution)/shard_map/all_to_all | solution.py:52
  122.4 43.0 %all-to-all-start.4 = ((bf16[64,3,2048]{2,1,0:T(4,128)(2,1)}), bf16[64,3,2048]{2,1,0:T(4,128)(2,1)}, u32[]{:S(2)}, u32[]{:S(2)}) async-start(bf16[64,3,2048]{2,1,0:T(4,128)(2,1)} %copy.219), calls=%async_computation.4 | async-start | bytes 2097152 | tf_op jit(solution)/shard_map/all_to_all | solution.py:45
  240.8 34.5 %all-to-all-start.7 = ((bf16[64,3,2048]{2,1,0:T(4,128)(2,1)}), bf16[64,3,2048]{2,1,0:T(4,128)(2,1)}, u32[]{:S(2)}, u32[]{:S(2)}) async-start(bf16[64,3,2048]{2,1,0:T(4,128)(2,1)} %copy.223), calls=%async_computation.7 | async-start | bytes 2097152 | tf_op jit(solution)/shard_map/all_to_all | solution.py:45
  287.7 31.1 %all-to-all-start.8 = ((bf16[64,3,2048]{2,1,0:T(4,128)(2,1)}), bf16[64,3,2048]{2,1,0:T(4,128)(2,1)}, u32[]{:S(2)}, u32[]{:S(2)}) async-start(bf16[64,3,2048]{2,1,0:T(4,128)(2,1)} %reshape.643), calls=%async_computation.8 | async-start | bytes 2097152 | tf_op jit(solution)/shard_map/all_to_all | solution.py:52
  345.1 32.7 %all-to-all-start.10 = ((bf16[64,3,2048]{2,1,0:T(4,128)(2,1)}), bf16[64,3,2048]{2,1,0:T(4,128)(2,1)}, u32[]{:S(2)}, u32[]{:S(2)}) async-start(bf16[64,3,2048]{2,1,0:T(4,128)(2,1)} %copy.227), calls=%async_computation.10 | async-start | bytes 2097152 | tf_op jit(solution)/shard_map/all_to_all | solution.py:45
  390.2 31.1 %all-to-all-start.11 = ((bf16[64,3,2048]{2,1,0:T(4,128)(2,1)}), bf16[64,3,2048]{2,1,0:T(4,128)(2,1)}, u32[]{:S(2)}, u32[]{:S(2)}) async-start(bf16[64,3,2048]{2,1,0:T(4,128)(2,1)} %reshape.645), calls=%async_computation.11 | async-start | bytes 2097152 | tf_op jit(solution)/shard_map/all_to_all | solution.py:52
  447.0 27.6 %all-to-all-start.13 = ((bf16[64,3,2048]{2,1,0:T(4,128)(2,1)}), bf16[64,3,2048]{2,1,0:T(4,128)(2,1)}, u32[]{:S(2)}, u32[]{:S(2)}) async-start(bf16[64,3,2048]{2,1,0:T(4,128)(2,1)} %copy.231), calls=%async_computation.13 | async-start | bytes 2097152 | tf_op jit(solution)/shard_map/all_to_all | solution.py:45
  479.9 30.7 %all-to-all-start.14 = ((bf16[64,3,2048]{2,1,0:T(4,128)(2,1)}), bf16[64,3,2048]{2,1,0:T(4,128)(2,1)}, u32[]{:S(2)}, u32[]{:S(2)}) async-start(bf16[64,3,2048]{2,1,0:T(4,128)(2,1)} %reshape.647), calls=%async_computation.14 | async-start | bytes 2097152 | tf_op jit(solution)/shard_map/all_to_all | solution.py:52
  536.3 28.2 %all-to-all-start.16 = ((bf16[64,3,2048]{2,1,0:T(4,128)(2,1)}), bf16[64,3,2048]{2,1,0:T(4,128)(2,1)}, u32[]{:S(2)}, u32[]{:S(2)}) async-start(bf16[64,3,2048]{2,1,0:T(4,128)(2,1)} %copy.235), calls=%async_computation.16 | async-start | bytes 2097152 | tf_op jit(solution)/shard_map/all_to_all | solution.py:45
  569.6 37.7 %all-to-all-start.17 = ((bf16[64,3,2048]{2,1,0:T(4,128)(2,1)}), bf16[64,3,2048]{2,1,0:T(4,128)(2,1)}, u32[]{:S(2)}, u32[]{:S(2)}) async-start(bf16[64,3,2048]{2,1,0:T(4,128)(2,1)} %reshape.649), calls=%async_computation.17 | async-start | bytes 2097152 | tf_op jit(solution)/shard_map/all_to_all | solution.py:52
  631.6 34.4 %all-to-all-start.19 = ((bf16[64,3,2048]{2,1,0:T(4,128)(2,1)}), bf16[64,3,2048]{2,1,0:T(4,128)(2,1)}, u32[]{:S(2)}, u32[]{:S(2)}) async-start(bf16[64,3,2048]{2,1,0:T(4,128)(2,1)} %copy.239), calls=%async_computation.19 | async-start | bytes 2097152 | tf_op jit(solution)/shard_map/all_to_all | solution.py:45
  694.6 27.6 %all-to-all-start.22 = ((bf16[64,3,2048]{2,1,0:T(4,128)(2,1)}), bf16[64,3,2048]{2,1,0:T(4,128)(2,1)}, u32[]{:S(2)}, u32[]{:S(2)}) async-start(bf16[64,3,2048]{2,1,0:T(4,128)(2,1)} %reshape.654), calls=%async_computation.22 | async-start | bytes 2097152 | tf_op jit(solution)/shard_map/all_to_all | solution.py:60
  744.6 34.2 %all-to-all-start.23 = ((bf16[64,3,2048]{2,1,0:T(4,128)(2,1)}), bf16[64,3,2048]{2,1,0:T(4,128)(2,1)}, u32[]{:S(2)}, u32[]{:S(2)}) async-start(bf16[64,3,2048]{2,1,0:T(4,128)(2,1)} %copy.251), calls=%async_computation.23 | async-start | bytes 2097152 | tf_op jit(solution)/shard_map/all_to_all | solution.py:56
  827.4 40.7 %all-to-all-start.25 = ((bf16[64,3,2048]{2,1,0:T(4,128)(2,1)}), bf16[64,3,2048]{2,1,0:T(4,128)(2,1)}, u32[]{:S(2)}, u32[]{:S(2)}) async-start(bf16[64,3,2048]{2,1,0:T(4,128)(2,1)} %copy.253), calls=%async_computation.25 | async-start | bytes 2097152 | tf_op jit(solution)/shard_map/all_to_all | solution.py:56
  922.4 36.3 %all-to-all-start.27 = ((bf16[64,3,2048]{2,1,0:T(4,128)(2,1)}), bf16[64,3,2048]{2,1,0:T(4,128)(2,1)}, u32[]{:S(2)}, u32[]{:S(2)}) async-start(bf16[64,3,2048]{2,1,0:T(4,128)(2,1)} %copy.255), calls=%async_computation.27 | async-start | bytes 2097152 | tf_op jit(solution)/shard_map/all_to_all | solution.py:56
  1012.4 36.3 %all-to-all-start.29 = ((bf16[64,3,2048]{2,1,0:T(4,128)(2,1)}), bf16[64,3,2048]{2,1,0:T(4,128)(2,1)}, u32[]{:S(2)}, u32[]{:S(2)}) async-start(bf16[64,3,2048]{2,1,0:T(4,128)(2,1)} %copy.257), calls=%async_computation.29 | async-start | bytes 2097152 | tf_op jit(solution)/shard_map/all_to_all | solution.py:56
  1090.1 24.7 %collective-permute-start.10 = (bf16[32,2048]{1,0:T(8,128)(2,1)S(1)}, bf16[32,2048]{1,0:T(8,128)(2,1)S(1)}, u32[]{:S(2)}, u32[]{:S(2)}) collective-permute-start(bf16[32,2048]{1,0:T(8,128)(2,1)S(1)} %get-tuple-element.782), channel_id=1, source_target_pairs={{8,0},{16,8},{24,16},{9,1},{17,9},{25,17},{10,2},{18,10},{26,18},{... | collective-permute-start | bytes 393224 | tf_op jit(solution)/shard_map/ppermute | solution.py:13
  1117.9 33.7 %all-to-all-start.31 = ((bf16[64,3,2048]{2,1,0:T(4,128)(2,1)}), bf16[64,3,2048]{2,1,0:T(4,128)(2,1)}, u32[]{:S(2)}, u32[]{:S(2)}) async-start(bf16[64,3,2048]{2,1,0:T(4,128)(2,1)} %copy.259), calls=%async_computation.31 | async-start | bytes 2097152 | tf_op jit(solution)/shard_map/all_to_all | solution.py:56
  1164.6 33.5 %all-to-all-start.32 = ((bf16[64,3,2048]{2,1,0:T(4,128)(2,1)}), bf16[64,3,2048]{2,1,0:T(4,128)(2,1)}, u32[]{:S(2)}, u32[]{:S(2)}) async-start(bf16[64,3,2048]{2,1,0:T(4,128)(2,1)} %reshape.664), calls=%async_computation.32 | async-start | bytes 2097152 | tf_op jit(solution)/shard_map/all_to_all | solution.py:60
  1211.5 31.9 %all-to-all-start.33 = ((bf16[64,3,2048]{2,1,0:T(4,128)(2,1)}), bf16[64,3,2048]{2,1,0:T(4,128)(2,1)}, u32[]{:S(2)}, u32[]{:S(2)}) async-start(bf16[64,3,2048]{2,1,0:T(4,128)(2,1)} %copy.261), calls=%async_computation.33 | async-start | bytes 2097152 | tf_op jit(solution)/shard_map/all_to_all | solution.py:56
  1243.3 29.7 %all-to-all-start.20 = ((bf16[64,3,2048]{2,1,0:T(4,128)(2,1)}), bf16[64,3,2048]{2,1,0:T(4,128)(2,1)}, u32[]{:S(2)}, u32[]{:S(2)}) async-start(bf16[64,3,2048]{2,1,0:T(4,128)(2,1)} %reshape.651), calls=%async_computation.20 | async-start | bytes 2097152 | tf_op jit(solution)/shard_map/all_to_all | solution.py:52
  1273.1 27.1 %all-to-all-start.34 = ((bf16[64,3,2048]{2,1,0:T(4,128)(2,1)}), bf16[64,3,2048]{2,1,0:T(4,128)(2,1)S(1)}, u32[]{:S(2)}, u32[]{:S(2)}) async-start(bf16[64,3,2048]{2,1,0:T(4,128)(2,1)} %reshape.666), calls=%async_computation.34 | async-start | bytes 2097152 | tf_op jit(solution)/shard_map/all_to_all | solution.py:60
  (51 other events, 667.9 us)
